TPU v7x, 128 devices: a whole 4x4x4 slice. The times are simulated.
128 devices in a mesh: row: 8 (over z, core), col: 16 (over y, x).
Axes of the slice: x: 4, y: 4, z: 4, core: 2. Of those that a mesh axis runs over, the one named last changes fastest.
Arguments:
- inputs: bfloat16 [512, 8192], P('row', 'col'), may hold values from -6 to 6
- grad_out: bfloat16 [512, 8192], P('row', 'col'), may hold values from -0.1796875 to 0.1796875
- gate_pre: bfloat16 [512, 28672], P('col', 'row'), may hold values from -6 to 6
- up_pre: bfloat16 [512, 28672], P('col', 'row'), may hold values from -6 to 6
- w_gate: bfloat16 [8192, 28672], P('col', 'row'), may hold values from -0.25 to 0.25
- w_up: bfloat16 [8192, 28672], P('col', 'row'), may hold values from -0.25 to 0.25
- w_down: bfloat16 [28672, 8192], P('row', 'col'), may hold values from -0.03125 to 0.03125
Outputs:
- grad_inputs: bfloat16 [512, 8192], P('row', 'col')
- grad_gate: bfloat16 [8192, 28672], P('col', 'row')
- grad_up: bfloat16 [8192, 28672], P('col', 'row')
- grad_down: bfloat16 [28672, 8192], P('row', 'col')
All inputs are finite; a program needn't handle non-finite values.
Results may differ from a plain program's by a relative error of at most 0.005.
Values may be sent and summed in bfloat16 or wider, within the bound.
A program may use at most 128 MiB of HBM per device.

v0:
```python
import jax
import jax.numpy as jnp
from jax import lax
from jax.sharding import PartitionSpec as P


def swiglu_back(gate_pre, up_pre, hidden_grad):
    gate_wide = gate_pre.astype(jnp.float32)
    up_wide = up_pre.astype(jnp.float32)
    logistic = jax.nn.sigmoid(gate_wide)
    swished = gate_wide * logistic
    hidden = (swished * up_wide).astype(jnp.bfloat16)
    up_grad = (hidden_grad * swished).astype(jnp.bfloat16)
    gate_grad = (hidden_grad * up_wide * logistic * (1.0 + gate_wide * (1.0 - logistic))).astype(
        jnp.bfloat16
    )
    return (hidden, gate_grad, up_grad)


def on_device(inputs, grad_out, gate_pre, up_pre, w_gate, w_up, w_down):
    last_last = (((1,), (1,)), ((), ()))
    first_first = (((0,), (0,)), ((), ()))
    inputs_all, grad_out_all = (
        lax.all_gather(inputs, "row", axis=0, tiled=True),
        lax.all_gather(grad_out, "row", axis=0, tiled=True),
    )
    hidden_grad = lax.psum_scatter(
        lax.dot_general(grad_out_all, w_down, last_last, preferred_element_type=jnp.float32),
        "col",
        scatter_dimension=0,
        tiled=True,
    )
    hidden, gate_grad, up_grad = swiglu_back(gate_pre, up_pre, hidden_grad)
    hidden_all, gate_grad_all, up_grad_all = (
        lax.all_gather(hidden, "col", axis=0, tiled=True),
        lax.all_gather(gate_grad, "col", axis=0, tiled=True),
        lax.all_gather(up_grad, "col", axis=0, tiled=True),
    )
    grad_down = lax.dot_general(
        hidden_all, grad_out_all, first_first, preferred_element_type=jnp.float32
    ).astype(jnp.bfloat16)
    grad_gate = lax.dot_general(
        inputs_all, gate_grad_all, first_first, preferred_element_type=jnp.float32
    ).astype(jnp.bfloat16)
    grad_up = lax.dot_general(
        inputs_all, up_grad_all, first_first, preferred_element_type=jnp.float32
    ).astype(jnp.bfloat16)
    summed = lax.dot_general(gate_grad_all, w_gate, last_last, preferred_element_type=jnp.float32)
    grad_inputs = lax.psum_scatter(
        summed + lax.dot_general(up_grad_all, w_up, last_last, preferred_element_type=jnp.float32),
        "row",
        scatter_dimension=0,
        tiled=True,
    ).astype(jnp.bfloat16)
    return (grad_inputs, grad_gate, grad_up, grad_down)


def solution(mesh):
    placed = (
        P("row", "col"),
        P("row", "col"),
        P("col", "row"),
        P("col", "row"),
        P("col", "row"),
        P("col", "row"),
        P("row", "col"),
    )
    return jax.shard_map(
        on_device,
        mesh=mesh,
        in_specs=placed,
        out_specs=(P("row", "col"), P("col", "row"), P("col", "row"), P("row", "col")),
        check_vma=False,
    )
```

profile of v0, /device:TPU:0, one launch (start us, length us, event | category | flops | bytes accessed | tf_op | source)
XLA Modules:
  0.0 309.3 jit_solution(8646618759056539256)
XLA Ops:
  7.2 0.0 reduce-scatter.3.cloned.1.call-start
  7.2 14.6 %all_gather.15 = bf16[512,512]{1,0:T(8,128)(2,1)S(1)} all-gather(bf16[64,512]{1,0:T(8,128)(2,1)} %param.8), channel_id=1, replica_groups=mesh['row'=8,'col'=16] {'row'}, dimensions={0}, use_global_device_ids=true | all-gather | bytes 589824 | tf_op jit(solution)/shard_map/all_gather | solution.py:25
  21.8 7.1 %fusion.10 = f32[512,3584]{1,0:T(8,128)} fusion(bf16[512,512]{1,0:T(8,128)(2,1)S(1)} %all_gather.15, bf16[3584,512]{1,0:T(8,128)(2,1)} %param.13), kind=kOutput, calls=%fused_computation.20 | convolution fusion | flops 1879048192 | bytes 11534336 | tf_op jit(solution)/shard_map/dot_general | solution.py:28
  28.9 0.0 copy-start
  28.9 0.0 copy-start.1
  28.9 0.0 reduce-scatter.3.cloned.1.call-update
  28.9 0.0 all-gather.4.cloned.1.call-start
  29.0 84.0 %reduce-scatter.3.cloned.1.call-done = f32[32,3584]{1,0:T(8,128)} async-done(((f32[512,3584]{1,0:T(8,128)}), f32[32,3584]{1,0:T(8,128)}) %reduce-scatter.3.cloned.1.call-update) | async-done | bytes 458768 | tf_op jit(solution)/shard_map/reduce_scatter | solution.py:27
  113.0 0.0 copy-done
  113.0 0.0 copy-done.1
  113.0 2.1 multiply_convert_fusion
  115.1 0.0 all-gather.4.cloned.1.call-update
  115.1 0.0 all-gather.6.cloned.1.call-start
  115.2 0.7 all-gather.6.cloned.1.call-update
  115.9 0.0 all-gather.8.cloned.1.call-start
  115.9 0.5 all-gather.8.cloned.1.call-update
  116.4 0.0 reduce-scatter.5.cloned.1.call-start
  116.5 48.4 %all-gather.4.cloned.1.call-done = bf16[512,3584]{1,0:T(8,128)(2,1)} async-done(((bf16[32,3584]{1,0:T(8,128)(2,1)}), bf16[512,3584]{1,0:T(8,128)(2,1)}) %all-gather.4.cloned.1.call-update) | async-done | bytes 3670032 | tf_op jit(solution)/shard_map/all_gather | solution.py:36
  164.9 5.2 %fusion.11 = f32[512,512]{1,0:T(8,128)S(1)} fusion(bf16[512,3584]{1,0:T(8,128)(2,1)} %all-gather.4.cloned.1.call-done, bf16[512,3584]{1,0:T(8,128)(2,1)} %param.11), kind=kOutput, calls=%fused_computation.21 | convolution fusion | flops 1879048192 | bytes 8388608 | tf_op jit(solution)/shard_map/dot_general | solution.py:48
  170.1 0.0 copy-start.2
  170.1 46.5 %all-gather.6.cloned.1.call-done = bf16[512,3584]{1,0:T(8,128)(2,1)} async-done(((bf16[32,3584]{1,0:T(8,128)(2,1)}), bf16[512,3584]{1,0:T(8,128)(2,1)}) %all-gather.6.cloned.1.call-update) | async-done | bytes 3670032 | tf_op jit(solution)/shard_map/all_gather | solution.py:37
  216.6 6.2 %convolution_add_fusion = f32[512,512]{1,0:T(8,128)} fusion(f32[512,512]{1,0:T(8,128)S(1)} %fusion.11, bf16[512,3584]{1,0:T(8,128)(2,1)} %all-gather.6.cloned.1.call-done, bf16[512,3584]{1,0:T(8,128)(2,1)} %param.12), kind=kOutput, calls=%fused_computation.5 | convolution fusion | flops 1879310336 | bytes 9437184 | tf_op jit(solution)/shard_map/dot_general | solution.py:50
  222.8 0.0 reduce-scatter.5.cloned.1.call-update
  222.8 0.0 copy-done.2
  222.8 13.8 %all_gather.18 = bf16[512,512]{1,0:T(8,128)(2,1)S(1)} all-gather(bf16[64,512]{1,0:T(8,128)(2,1)S(1)} %copy-done.2), channel_id=1, replica_groups=mesh['row'=8,'col'=16] {'row'}, dimensions={0}, use_global_device_ids=true | all-gather | bytes 589824 | tf_op jit(solution)/shard_map/all_gather | solution.py:24
  236.6 6.0 %fusion = bf16[512,3584]{0,1:T(8,128)(2,1)} fusion(bf16[512,3584]{1,0:T(8,128)(2,1)} %all-gather.4.cloned.1.call-done, bf16[512,512]{1,0:T(8,128)(2,1)S(1)} %all_gather.18), kind=kOutput, calls=%fused_computation.3 | convolution fusion | flops 1880883200 | bytes 7864320 | tf_op jit(solution)/shard_map/dot_general | solution.py:42
  242.6 5.9 %copy.11 = bf16[512,3584]{1,0:T(8,128)(2,1)} copy(bf16[512,3584]{0,1:T(8,128)(2,1)} %fusion) | data formatting | bytes 7340032
  248.5 6.0 %fusion.1 = bf16[512,3584]{0,1:T(8,128)(2,1)} fusion(bf16[512,3584]{1,0:T(8,128)(2,1)} %all-gather.6.cloned.1.call-done, bf16[512,512]{1,0:T(8,128)(2,1)S(1)} %all_gather.18), kind=kOutput, calls=%fused_computation.4 | convolution fusion | flops 1880883200 | bytes 7864320 | tf_op jit(solution)/shard_map/dot_general | solution.py:45
  254.5 5.9 %copy.12 = bf16[512,3584]{1,0:T(8,128)(2,1)} copy(bf16[512,3584]{0,1:T(8,128)(2,1)} %fusion.1) | data formatting | bytes 7340032
  260.5 7.1 %all-gather.8.cloned.1.call-done = bf16[512,3584]{1,0:T(8,128)(2,1)} async-done(((bf16[32,3584]{1,0:T(8,128)(2,1)}), bf16[512,3584]{1,0:T(8,128)(2,1)}) %all-gather.8.cloned.1.call-update) | async-done | bytes 3670032 | tf_op jit(solution)/shard_map/all_gather | solution.py:35
  267.6 6.0 %convolution_convert_fusion = bf16[3584,512]{1,0:T(8,128)(2,1)} fusion(bf16[512,3584]{1,0:T(8,128)(2,1)} %all-gather.8.cloned.1.call-done, bf16[512,512]{1,0:T(8,128)(2,1)S(1)} %all_gather.15), kind=kOutput, calls=%fused_computation | convolution fusion | flops 1880883200 | bytes 7864320 | tf_op jit(solution)/shard_map/dot_general | solution.py:39
  273.6 27.6 %reduce-scatter.5.cloned.1.call-done = f32[64,512]{1,0:T(8,128)} async-done(((f32[512,512]{1,0:T(8,128)}), f32[64,512]{1,0:T(8,128)}) %reduce-scatter.5.cloned.1.call-update) | async-done | bytes 131088 | tf_op jit(solution)/shard_map/reduce_scatter | solution.py:49
  301.2 1.5 convert_element_type.37
Async XLA Ops:
  7.2 105.8 %reduce-scatter.3.cloned.1.call-start = ((), (), s32[]{:S(2)}) async-start(), calls=%async_computation.2 | async-start | bytes 7798784 | tf_op jit(solution)/shard_map/reduce_scatter | solution.py:27
  28.9 84.1 %copy-start = (bf16[32,3584]{1,0:T(8,128)(2,1)S(1)}, bf16[32,3584]{1,0:T(8,128)(2,1)}, u32[]{:S(2)}) copy-start(bf16[32,3584]{1,0:T(8,128)(2,1)} %param.9) | copy-start | bytes 688132
  28.9 84.1 %copy-start.1 = (bf16[32,3584]{1,0:T(8,128)(2,1)S(1)}, bf16[32,3584]{1,0:T(8,128)(2,1)}, u32[]{:S(2)}) copy-start(bf16[32,3584]{1,0:T(8,128)(2,1)} %param.10) | copy-start | bytes 688132
  28.9 135.9 %all-gather.4.cloned.1.call-start = ((), (), s32[]{:S(2)}) async-start(), calls=%async_computation.3 | async-start | bytes 3899392 | tf_op jit(solution)/shard_map/all_gather | solution.py:36
  115.1 101.5 %all-gather.6.cloned.1.call-start = ((), (), s32[]{:S(2)}) async-start(), calls=%async_computation.4 | async-start | bytes 3899392 | tf_op jit(solution)/shard_map/all_gather | solution.py:37
  115.9 151.7 %all-gather.8.cloned.1.call-start = ((), (), s32[]{:S(2)}) async-start(), calls=%async_computation.6 | async-start | bytes 3899392 | tf_op jit(solution)/shard_map/all_gather | solution.py:35
  116.4 184.8 %reduce-scatter.5.cloned.1.call-start = ((), (), s32[]{:S(2)}) async-start(), calls=%async_computation.5 | async-start | bytes 1179648 | tf_op jit(solution)/shard_map/reduce_scatter | solution.py:49
  170.1 52.7 %copy-start.2 = (bf16[64,512]{1,0:T(8,128)(2,1)S(1)}, bf16[64,512]{1,0:T(8,128)(2,1)}, u32[]{:S(2)}) copy-start(bf16[64,512]{1,0:T(8,128)(2,1)} %param.7) | copy-start | bytes 196612
Sparse Core Ops, SparseCore 0:
  29.0 83.9 reduce-scatter.2
  115.9 48.8 all-gather.3
  167.8 48.7 all-gather.5
  218.8 48.7 all-gather.7
  270.0 31.2 reduce-scatter.4
where the time goes:
time: 310 us; the launch traced here: 309 us
  waiting for transfers between devices  215 us (69%)
  matrix products  36.5 us (12%)
  blocking collectives  28.4 us (9%)
  between operations  13.8 us (4%)
  local copies, waits for them, and re-layouts  11.9 us (4%)
  other arithmetic  3.61 us (1%)
    reduce_scatter x1, waiting for transfers between devices, on_device(): lax.psum_scatter(lax.dot_general(grad_out_all, w_down, last_last, preferr...  84 us
    all_gather x1, waiting for transfers between devices, on_device(): lax.all_gather(gate_grad, 'col', axis=0, tiled=True)  48.4 us
    all_gather x1, waiting for transfers between devices, on_device(): lax.all_gather(up_grad, 'col', axis=0, tiled=True)  46.5 us
    reduce_scatter x1, waiting for transfers between devices, on_device(): lax.psum_scatter(summed + lax.dot_general(up_grad_all, w_up, last_last, p...  27.6 us
    all_gather x1, blocking collectives, on_device(): lax.all_gather(grad_out, 'row', axis=0, tiled=True)  14.6 us
    all_gather x1, blocking collectives, on_device(): lax.all_gather(inputs, 'row', axis=0, tiled=True)  13.8 us
    unnamed x8, local copies, waits for them, and re-layouts  11.9 us
    all_gather x1, waiting for transfers between devices, on_device(): lax.all_gather(hidden, 'col', axis=0, tiled=True)  7.13 us
  transfers between devices with their start and end apart: 5, of which 5 were waited for; matrix products, arithmetic and copies ran while one was open for 13% of the time, Pallas kernels for 0%

commit v1 on v0

--- a/solution.py
+++ b/solution.py
@@ -33,7 +33,9 @@
     hidden, gate_grad, up_grad = swiglu_back(gate_pre, up_pre, hidden_grad)
     hidden_all, gate_grad_all, up_grad_all = (
         lax.all_gather(hidden, "col", axis=0, tiled=True),
-        lax.all_gather(gate_grad, "col", axis=0, tiled=True),
+        jnp.concatenate(
+            lax.all_to_all(jnp.stack([gate_grad] * lax.axis_size("col")), "col", 0, 0), axis=0
+        ),
         lax.all_gather(up_grad, "col", axis=0, tiled=True),
     )
     grad_down = lax.dot_general(

time: 310 us -> 282 us (0.910)
  waiting for transfers between devices: 215 us -> 134 us
  blocking collectives: 28.4 us -> 82.1 us
    all_to_all x0 -> x1, blocking collectives: none -> 53.7 us  [on_device(): lax.all_to_all(jnp.stack([gate_grad] * lax.axis_size('col')), 'col', 0, 0)]
    all_gather x1 -> x0, waiting for transfers between devices: 48.4 us -> none  [on_device(): lax.all_gather(gate_grad, 'col', axis=0, tiled=True)]
    all_gather x1, waiting for transfers between devices: 46.5 us -> 14.2 us  [on_device(): lax.all_gather(up_grad, 'col', axis=0, tiled=True)]
    dot_general x1, matrix products: 5.24 us -> 2.08 us  [on_device(): lax.dot_general(gate_grad_all, w_gate, last_last, preferred_element_type=...]
    unnamed x8 -> x12, local copies, waits for them, and re-layouts: 11.9 us -> 13.7 us
  transfers between devices with their start and end apart: 5 -> 4, of which waited for: 5 -> 4; matrix products, arithmetic and copies ran while one was open for 13% -> 14% of each run, Pallas kernels for 0% -> 0%
where the time goes in v1:
time: 282 us; the launch traced here: 281 us
  waiting for transfers between devices  134 us (48%)
  blocking collectives  82.1 us (29%)
  matrix products  33.5 us (12%)
  local copies, waits for them, and re-layouts  14 us (5%)
  between operations  13.8 us (5%)
  other arithmetic  3.61 us (1%)
    reduce_scatter x1, waiting for transfers between devices, on_device(): lax.psum_scatter(lax.dot_general(grad_out_all, w_down, last_last, preferr...  84.3 us
    all_to_all x1, blocking collectives, on_device(): lax.all_to_all(jnp.stack([gate_grad] * lax.axis_size('col')), 'col', 0, 0)  53.7 us
    reduce_scatter x1, waiting for transfers between devices, on_device(): lax.psum_scatter(summed + lax.dot_general(up_grad_all, w_up, last_last, p...  27.7 us
    all_gather x1, blocking collectives, on_device(): lax.all_gather(grad_out, 'row', axis=0, tiled=True)  14.6 us
    all_gather x1, waiting for transfers between devices, on_device(): lax.all_gather(up_grad, 'col', axis=0, tiled=True)  14.2 us
    all_gather x1, blocking collectives, on_device(): lax.all_gather(inputs, 'row', axis=0, tiled=True)  13.8 us
    unnamed x12, local copies, waits for them, and re-layouts  13.7 us
    all_gather x1, waiting for transfers between devices, on_device(): lax.all_gather(hidden, 'col', axis=0, tiled=True)  7.18 us
  transfers between devices with their start and end apart: 4, of which 4 were waited for; matrix products, arithmetic and copies ran while one was open for 14% of the time, Pallas kernels for 0%

profile of v1, /device:TPU:0, one launch (start us, length us, event | category | flops | bytes accessed | tf_op | source)
XLA Modules:
  0.0 281.4 jit_solution(453135593003724417)
XLA Ops:
  7.2 0.0 reduce-scatter.3.cloned.1.call-start
  7.2 14.6 %all_gather.12 = bf16[512,512]{1,0:T(8,128)(2,1)S(1)} all-gather(bf16[64,512]{1,0:T(8,128)(2,1)} %param.8), channel_id=1, replica_groups=mesh['row'=8,'col'=16] {'row'}, dimensions={0}, use_global_device_ids=true | all-gather | bytes 589824 | tf_op jit(solution)/shard_map/all_gather | solution.py:25
  21.8 7.1 %fusion.10 = f32[512,3584]{1,0:T(8,128)} fusion(bf16[512,512]{1,0:T(8,128)(2,1)S(1)} %all_gather.12, bf16[3584,512]{1,0:T(8,128)(2,1)} %param.13), kind=kOutput, calls=%fused_computation.20 | convolution fusion | flops 1879048192 | bytes 11534336 | tf_op jit(solution)/shard_map/dot_general | solution.py:28
  28.9 0.0 copy-start.1
  28.9 0.0 copy-start.2
  28.9 0.0 reduce-scatter.3.cloned.1.call-update
  28.9 0.0 all-gather.3.cloned.1.call-start
  29.0 84.3 %reduce-scatter.3.cloned.1.call-done = f32[32,3584]{1,0:T(8,128)} async-done(((f32[512,3584]{1,0:T(8,128)}), f32[32,3584]{1,0:T(8,128)}) %reduce-scatter.3.cloned.1.call-update) | async-done | bytes 458768 | tf_op jit(solution)/shard_map/reduce_scatter | solution.py:27
  113.3 0.0 copy-done.1
  113.3 0.0 copy-done.2
  113.3 2.1 multiply_convert_fusion
  115.4 0.0 all-gather.3.cloned.1.call-update
  115.4 0.0 all-gather.5.cloned.1.call-start
  115.4 0.7 all-gather.5.cloned.1.call-update
  116.1 0.0 reduce-scatter.5.cloned.1.call-start
  116.2 0.3 stack.2
  116.5 0.0 copy-start.4
  116.5 53.7 %all_to_all.5 = bf16[16,32,3584]{2,1,0:T(8,128)(2,1)S(1)} all-to-all(bf16[16,32,3584]{2,1,0:T(8,128)(2,1)S(1)} %stack.2), channel_id=1, replica_groups=mesh['row'=8,'col'=16] {'col'}, dimensions={0} | all-to-all | bytes 7340032 | tf_op jit(solution)/shard_map/all_to_all | solution.py:37
  170.3 0.0 copy-start
  170.3 1.8 copy-done
  172.1 0.0 copy-done.4
  172.1 2.1 fusion.11
  174.2 0.0 copy-start.3
  174.2 14.2 %all-gather.3.cloned.1.call-done = bf16[512,3584]{1,0:T(8,128)(2,1)} async-done(((bf16[32,3584]{1,0:T(8,128)(2,1)}), bf16[512,3584]{1,0:T(8,128)(2,1)}) %all-gather.3.cloned.1.call-update) | async-done | bytes 3670032 | tf_op jit(solution)/shard_map/all_gather | solution.py:39
  188.5 6.3 %convolution_add_fusion = f32[512,512]{1,0:T(8,128)} fusion(f32[512,512]{1,0:T(8,128)S(1)} %fusion.11, bf16[512,3584]{1,0:T(8,128)(2,1)} %all-gather.3.cloned.1.call-done, bf16[512,3584]{1,0:T(8,128)(2,1)} %param.12), kind=kOutput, calls=%fused_computation.5 | convolution fusion | flops 1879310336 | bytes 9437184 | tf_op jit(solution)/shard_map/dot_general | solution.py:52
  194.7 0.0 reduce-scatter.5.cloned.1.call-update
  194.8 0.0 copy-done.3
  194.8 13.8 %all_gather.14 = bf16[512,512]{1,0:T(8,128)(2,1)S(1)} all-gather(bf16[64,512]{1,0:T(8,128)(2,1)S(1)} %copy-done.3), channel_id=1, replica_groups=mesh['row'=8,'col'=16] {'row'}, dimensions={0}, use_global_device_ids=true | all-gather | bytes 589824 | tf_op jit(solution)/shard_map/all_gather | solution.py:24
  208.5 6.0 %fusion = bf16[512,3584]{0,1:T(8,128)(2,1)} fusion(bf16[512,3584]{1,0:T(8,128)(2,1)} %bitcast.18, bf16[512,512]{1,0:T(8,128)(2,1)S(1)} %all_gather.14), kind=kOutput, calls=%fused_computation.3 | convolution fusion | flops 1880883200 | bytes 7864320 | tf_op jit(solution)/shard_map/dot_general | solution.py:44
  214.5 5.9 %copy.11 = bf16[512,3584]{1,0:T(8,128)(2,1)} copy(bf16[512,3584]{0,1:T(8,128)(2,1)} %fusion) | data formatting | bytes 7340032
  220.4 6.1 %fusion.1 = bf16[512,3584]{0,1:T(8,128)(2,1)} fusion(bf16[512,3584]{1,0:T(8,128)(2,1)} %all-gather.3.cloned.1.call-done, bf16[512,512]{1,0:T(8,128)(2,1)S(1)} %all_gather.14), kind=kOutput, calls=%fused_computation.4 | convolution fusion | flops 1880883200 | bytes 7864320 | tf_op jit(solution)/shard_map/dot_general | solution.py:47
  226.5 5.9 %copy.12 = bf16[512,3584]{1,0:T(8,128)(2,1)} copy(bf16[512,3584]{0,1:T(8,128)(2,1)} %fusion.1) | data formatting | bytes 7340032
  232.4 7.2 %all-gather.5.cloned.1.call-done = bf16[512,3584]{1,0:T(8,128)(2,1)} async-done(((bf16[32,3584]{1,0:T(8,128)(2,1)}), bf16[512,3584]{1,0:T(8,128)(2,1)}) %all-gather.5.cloned.1.call-update) | async-done | bytes 3670032 | tf_op jit(solution)/shard_map/all_gather | solution.py:35
  239.6 6.0 %convolution_convert_fusion = bf16[3584,512]{1,0:T(8,128)(2,1)} fusion(bf16[512,3584]{1,0:T(8,128)(2,1)} %all-gather.5.cloned.1.call-done, bf16[512,512]{1,0:T(8,128)(2,1)S(1)} %all_gather.12), kind=kOutput, calls=%fused_computation | convolution fusion | flops 1880883200 | bytes 7864320 | tf_op jit(solution)/shard_map/dot_general | solution.py:41
  245.6 27.7 %reduce-scatter.5.cloned.1.call-done = f32[64,512]{1,0:T(8,128)} async-done(((f32[512,512]{1,0:T(8,128)}), f32[64,512]{1,0:T(8,128)}) %reduce-scatter.5.cloned.1.call-update) | async-done | bytes 131088 | tf_op jit(solution)/shard_map/reduce_scatter | solution.py:51
  273.3 1.5 convert_element_type.37
Async XLA Ops:
  7.2 106.1 %reduce-scatter.3.cloned.1.call-start = ((), (), s32[]{:S(2)}) async-start(), calls=%async_computation.3 | async-start | bytes 7798784 | tf_op jit(solution)/shard_map/reduce_scatter | solution.py:27
  28.9 84.4 %copy-start.1 = (bf16[32,3584]{1,0:T(8,128)(2,1)S(1)}, bf16[32,3584]{1,0:T(8,128)(2,1)}, u32[]{:S(2)}) copy-start(bf16[32,3584]{1,0:T(8,128)(2,1)} %param.9) | copy-start | bytes 688132
  28.9 84.4 %copy-start.2 = (bf16[32,3584]{1,0:T(8,128)(2,1)S(1)}, bf16[32,3584]{1,0:T(8,128)(2,1)}, u32[]{:S(2)}) copy-start(bf16[32,3584]{1,0:T(8,128)(2,1)} %param.10) | copy-start | bytes 688132
  28.9 159.5 %all-gather.3.cloned.1.call-start = ((), (), s32[]{:S(2)}) async-start(), calls=%async_computation.4 | async-start | bytes 3899392 | tf_op jit(solution)/shard_map/all_gather | solution.py:39
  115.4 124.2 %all-gather.5.cloned.1.call-start = ((), (), s32[]{:S(2)}) async-start(), calls=%async_computation.6 | async-start | bytes 3899392 | tf_op jit(solution)/shard_map/all_gather | solution.py:35
  116.1 157.2 %reduce-scatter.5.cloned.1.call-start = ((), (), s32[]{:S(2)}) async-start(), calls=%async_computation.5 | async-start | bytes 1179648 | tf_op jit(solution)/shard_map/reduce_scatter | solution.py:51
  116.5 55.6 %copy-start.4 = (bf16[512,3584]{1,0:T(8,128)(2,1)S(1)}, bf16[512,3584]{1,0:T(8,128)(2,1)}, u32[]{:S(2)}) copy-start(bf16[512,3584]{1,0:T(8,128)(2,1)} %param.11) | copy-start | bytes 11010052
  170.3 1.8 copy-start
  174.2 20.5 %copy-start.3 = (bf16[64,512]{1,0:T(8,128)(2,1)S(1)}, bf16[64,512]{1,0:T(8,128)(2,1)}, u32[]{:S(2)}) copy-start(bf16[64,512]{1,0:T(8,128)(2,1)} %param.7) | copy-start | bytes 196612
Sparse Core Ops, SparseCore 0:
  29.1 84.2 reduce-scatter.2
  116.2 72.1 all-gather.2
  190.8 48.7 all-gather.4
  242.0 31.2 reduce-scatter.4
